TPU v7x, 32 devices: a whole 2x2x4 slice. The times are simulated.
32 devices in a mesh: grp: 2 (over x), ctx: 4 (over z), wsh: 4 (over y, core).
Axes of the slice: x: 2, y: 2, z: 4, core: 2. Of those that a mesh axis runs over, the one named last changes fastest.
Arguments:
- inputs: bfloat16 [2, 4, 2048, 1024], P('grp', 'wsh', 'ctx'), may hold values from -6 to 6
- w_qkv: bfloat16 [1024, 3072], P('wsh'), may hold values from -0.1875 to 0.1875
- w_out: bfloat16 [1024, 1024], P('wsh'), may hold values from -0.1875 to 0.1875
- w_up: bfloat16 [1024, 4096], P('wsh'), may hold values from -0.1875 to 0.1875
- w_down: bfloat16 [4096, 1024], P('wsh'), may hold values from -0.09375 to 0.09375
- norm_gains: float32 [4, 1024], replicated, may hold values from 0.5 to 1.5
- norm_biases: float32 [4, 1024], replicated, may hold values from -2 to 2
- block_map: int32 [2, 4, 4, 2], P('grp', 'wsh', 'ctx'), may hold values from 0 to 1024, as said below
- out_grad: bfloat16 [2, 4, 2048, 1024], P('grp', 'wsh', 'ctx'), may hold values from -6 to 6
Outputs:
- output: bfloat16 [2, 4, 2048, 1024], P('grp', 'wsh', 'ctx')
- input_grad: float32 [2, 4, 2048, 1024], P('grp', 'wsh', 'ctx')
- grad_qkv: float32 [1024, 3072], P('wsh')
- grad_attn_out: float32 [1024, 1024], P('wsh')
- grad_up: float32 [1024, 4096], P('wsh')
- grad_down: float32 [4096, 1024], P('wsh')
- grad_gains: float32 [4, 1024], replicated
- grad_biases: float32 [4, 1024], replicated
Inputs may be any that keep to these rules, and one draw needn't show every extreme that they name: `block_map`: for each grp and wsh index the 4 context blocks are the 2 prompt blocks (sequence 0, first positions 0, 512, 1024 and so on) and one block of each continuation 1 to 4 // 2 (first position 1024), in an order drawn for each family.
All inputs are finite; a program needn't handle non-finite values.
Results may differ from a plain program's by a relative error of at most 0.017.
Values may be sent and summed in bfloat16 or wider, within the bound.
A program may use at most 384 MiB of HBM per device.

v0:
```python
import math
import jax
import jax.numpy as jnp
from jax import lax
from jax.sharding import PartitionSpec as P

D = 1024
HEADS = 16
DH = 64
BLK = 512
EPS = 1e-05
ALPHA = 32.0
NEG = -1e30


def layer_norm(values, gain_row, bias_row):
    centre = values - jnp.mean(values, axis=-1, keepdims=True)
    spread = jnp.mean(centre * centre, axis=-1, keepdims=True)
    return centre * lax.rsqrt(spread + EPS) * gain_row + bias_row


def gelu_tanh(values):
    return jax.nn.gelu(values, approximate=True)


def contract_last(left_side, right_side):
    return lax.dot_general(
        left_side, right_side, (((1,), (1,)), ((), ())), preferred_element_type=jnp.float32
    )


def contract_rows(left_side, right_side):
    return lax.dot_general(
        left_side, right_side, (((0,), (0,)), ((), ())), preferred_element_type=jnp.float32
    )


def allowed(query_tags, key_tags):
    same_doc = (key_tags[None, :, 0] == query_tags[:, None, 0]) | (key_tags[None, :, 0] == 0)
    return same_doc & (key_tags[None, :, 1] <= query_tags[:, None, 1])


def scores(queries, key_block, permit):
    raw_scores = jnp.einsum("qhd,khd->hqk", queries, key_block, preferred_element_type=jnp.float32)
    return jnp.where(permit[None], raw_scores * ALPHA, NEG)


def no_output(step_rows):
    return None


def zero_terms(step_rows):
    zero_rows = jnp.zeros((step_rows, HEADS, DH), jnp.float32)
    return (zero_rows, zero_rows)


def sweep_blocks(members, query_tags, state, update, blank):
    total_rows = members[0].shape[0]
    limit_rows = max(query_tags.shape[0], 512)
    block_count = total_rows // limit_rows
    stacked = tuple(
        (member.reshape((block_count, limit_rows) + member.shape[1:]) for member in members)
    )

    def advance(held_state, pieces):
        permit = allowed(query_tags, pieces[-1])

        def active(inner_state):
            return update(inner_state, pieces, permit)

        def passive(inner_state):
            return (inner_state, blank(limit_rows))

        return lax.cond(jnp.any(permit), active, passive, held_state)

    return lax.scan(advance, state, stacked)


def normaliser_update(queries):

    def update(held_state, pieces, permit):
        top_score, exp_total = held_state
        logits = scores(queries, pieces[0], permit)
        new_top = jnp.maximum(top_score, jnp.max(logits, axis=-1))
        kept_exp = jnp.where(permit[None], jnp.exp(logits - new_top[..., None]), 0.0)
        exp_total = exp_total * jnp.exp(top_score - new_top) + jnp.sum(kept_exp, axis=-1)
        return ((new_top, exp_total), None)

    return update


def output_update(queries, log_total):

    def update(held_state, pieces, permit):
        logits = scores(queries, pieces[0], permit)
        weights_low = jnp.where(permit[None], jnp.exp(logits - log_total[..., None]), 0.0).astype(
            jnp.bfloat16
        )
        return (
            held_state
            + jnp.einsum(
                "hqk,khd->qhd", weights_low, pieces[1], preferred_element_type=jnp.float32
            ),
            None,
        )

    return update


def inner_update(queries, log_total, grad_out_low):

    def update(held_state, pieces, permit):
        logits = scores(queries, pieces[0], permit)
        probs_full = jnp.where(permit[None], jnp.exp(logits - log_total[..., None]), 0.0)
        grad_probs = jnp.einsum(
            "qhd,khd->hqk", grad_out_low, pieces[1], preferred_element_type=jnp.float32
        )
        return (held_state + jnp.sum(probs_full * grad_probs, axis=-1), None)

    return update


def gradient_update(queries, log_total, grad_out_low, inner_sum):

    def update(held_state, pieces, permit):
        logits = scores(queries, pieces[0], permit)
        probs_full = jnp.where(permit[None], jnp.exp(logits - log_total[..., None]), 0.0)
        grad_probs = jnp.einsum(
            "qhd,khd->hqk", grad_out_low, pieces[1], preferred_element_type=jnp.float32
        )
        grad_logits = (probs_full * (grad_probs - inner_sum[..., None]) * ALPHA).astype(
            jnp.bfloat16
        )
        new_state = held_state + jnp.einsum(
            "hqk,khd->qhd", grad_logits, pieces[0], preferred_element_type=jnp.float32
        )
        key_term = jnp.einsum(
            "hqk,qhd->khd", grad_logits, queries, preferred_element_type=jnp.float32
        )
        value_term = jnp.einsum(
            "hqk,qhd->khd",
            probs_full.astype(jnp.bfloat16),
            grad_out_low,
            preferred_element_type=jnp.float32,
        )
        return (new_state, (key_term, value_term))

    return update


def per_device(inputs, w_qkv, w_out, w_up, w_down, norm_gains, norm_biases, block_map, out_grad):
    query_scale = 1.0 / (ALPHA * math.sqrt(DH))
    tokens = inputs.reshape(BLK, D).astype(jnp.float32)
    full_qkv, full_out, full_up, full_down = (
        lax.all_gather(w_qkv, "wsh", axis=0, tiled=True),
        lax.all_gather(w_out, "wsh", axis=0, tiled=True),
        lax.all_gather(w_up, "wsh", axis=0, tiled=True),
        lax.all_gather(w_down, "wsh", axis=0, tiled=True),
    )
    block_entry = block_map.reshape(2)
    local_tags = jnp.stack(
        [
            jnp.full((BLK,), block_entry[0], jnp.int32),
            block_entry[1] + jnp.arange(BLK, dtype=jnp.int32),
        ],
        axis=1,
    )
    first_norm, first_back = jax.vjp(layer_norm, tokens, norm_gains[0], norm_biases[0])
    normed_low = first_norm.astype(jnp.bfloat16)
    projected = jnp.dot(normed_low, full_qkv, preferred_element_type=jnp.float32)
    queries = (projected[:, :D] * query_scale).astype(jnp.bfloat16).reshape(BLK, HEADS, DH)
    key_local = projected[:, D : 2 * D].astype(jnp.bfloat16)
    value_local = projected[:, 2 * D :].astype(jnp.bfloat16)
    start_top = (jnp.full((HEADS, BLK), NEG, jnp.float32), jnp.zeros((HEADS, BLK), jnp.float32))
    start_out = jnp.zeros((BLK, HEADS, DH), jnp.float32)
    key_all, value_all, tag_all = (
        lax.all_gather(key_local, "ctx", axis=0, tiled=True),
        lax.all_gather(value_local, "ctx", axis=0, tiled=True),
        lax.all_gather(local_tags, "ctx", axis=0, tiled=True),
    )
    key_heads = key_all.reshape(-1, HEADS, DH)
    value_heads = value_all.reshape(-1, HEADS, DH)
    top_score, exp_total = sweep_blocks(
        (key_heads, tag_all), local_tags, start_top, normaliser_update(queries), no_output
    )[0]
    log_total = top_score + jnp.log(exp_total)
    attended = sweep_blocks(
        (key_heads, value_heads, tag_all),
        local_tags,
        start_out,
        output_update(queries, log_total),
        no_output,
    )[0]
    attn_low = attended.reshape(BLK, D).astype(jnp.bfloat16)
    branch = jnp.dot(attn_low, full_out, preferred_element_type=jnp.float32)
    post_attn, attn_back = jax.vjp(layer_norm, branch, norm_gains[1], norm_biases[1])
    hidden = tokens + post_attn
    pre_ffn, ffn_back = jax.vjp(layer_norm, hidden, norm_gains[2], norm_biases[2])
    ffn_low = pre_ffn.astype(jnp.bfloat16)
    upward = jnp.dot(ffn_low, full_up, preferred_element_type=jnp.float32)
    activated, gelu_back = jax.vjp(gelu_tanh, upward)
    active_low = activated.astype(jnp.bfloat16)
    downward = jnp.dot(active_low, full_down, preferred_element_type=jnp.float32)
    post_ffn, post_back = jax.vjp(layer_norm, downward, norm_gains[3], norm_biases[3])
    result = (hidden + post_ffn).astype(jnp.bfloat16).reshape(1, 1, BLK, D)
    seed_grad = out_grad.reshape(BLK, D).astype(jnp.float32)
    grad_down_in, gain_grad3, bias_grad3 = post_back(seed_grad)
    down_low = grad_down_in.astype(jnp.bfloat16)
    grad_active = contract_last(down_low, full_down)
    up_low = gelu_back(grad_active)[0].astype(jnp.bfloat16)
    grad_pre_ffn, gain_grad2, bias_grad2 = ffn_back(contract_last(up_low, full_up))
    grad_hidden = seed_grad + grad_pre_ffn
    grad_branch, gain_grad1, bias_grad1 = attn_back(grad_hidden)
    branch_low = grad_branch.astype(jnp.bfloat16)
    grad_out_low = contract_last(branch_low, full_out).astype(jnp.bfloat16).reshape(BLK, HEADS, DH)
    members = (key_heads, value_heads, tag_all)
    inner_sum = sweep_blocks(
        members,
        local_tags,
        jnp.zeros((HEADS, BLK), jnp.float32),
        inner_update(queries, log_total, grad_out_low),
        no_output,
    )[0]
    grad_queries, key_value_terms = sweep_blocks(
        members,
        local_tags,
        start_out,
        gradient_update(queries, log_total, grad_out_low, inner_sum),
        zero_terms,
    )
    key_terms = key_value_terms[0].reshape(-1, D)
    value_terms = key_value_terms[1].reshape(-1, D)
    key_grad, value_grad = (
        lax.psum_scatter(
            key_terms.astype(jnp.bfloat16), "ctx", scatter_dimension=0, tiled=True
        ).astype(jnp.float32),
        lax.psum_scatter(
            value_terms.astype(jnp.bfloat16), "ctx", scatter_dimension=0, tiled=True
        ).astype(jnp.float32),
    )
    qkv_low = jnp.concatenate(
        [
            grad_queries.reshape(BLK, D).astype(jnp.bfloat16) * query_scale,
            key_grad.astype(jnp.bfloat16),
            value_grad.astype(jnp.bfloat16),
        ],
        axis=1,
    )
    grad_tokens, gain_grad0, bias_grad0 = first_back(contract_last(qkv_low, full_qkv))
    grad_input = (grad_hidden + grad_tokens).reshape(1, 1, BLK, D)
    term_qkv = contract_rows(normed_low, qkv_low)
    term_out = contract_rows(attn_low, branch_low)
    term_up = contract_rows(ffn_low, up_low)
    term_down = contract_rows(active_low, down_low)
    shard_qkv, shard_out, shard_up, shard_down = (
        lax.psum_scatter(
            term_qkv.astype(jnp.bfloat16), "wsh", scatter_dimension=0, tiled=True
        ).astype(jnp.float32),
        lax.psum_scatter(
            term_out.astype(jnp.bfloat16), "wsh", scatter_dimension=0, tiled=True
        ).astype(jnp.float32),
        lax.psum_scatter(
            term_up.astype(jnp.bfloat16), "wsh", scatter_dimension=0, tiled=True
        ).astype(jnp.float32),
        lax.psum_scatter(
            term_down.astype(jnp.bfloat16), "wsh", scatter_dimension=0, tiled=True
        ).astype(jnp.float32),
    )
    summed_qkv, summed_out, summed_up, summed_down = (
        lax.psum(shard_qkv.astype(jnp.bfloat16), ("grp", "ctx")).astype(jnp.float32),
        lax.psum(shard_out.astype(jnp.bfloat16), ("grp", "ctx")).astype(jnp.float32),
        lax.psum(shard_up.astype(jnp.bfloat16), ("grp", "ctx")).astype(jnp.float32),
        lax.psum(shard_down.astype(jnp.bfloat16), ("grp", "ctx")).astype(jnp.float32),
    )
    gain_stack = jnp.stack([gain_grad0, gain_grad1, gain_grad2, gain_grad3])
    bias_stack = jnp.stack([bias_grad0, bias_grad1, bias_grad2, bias_grad3])
    gain_total, bias_total = lax.psum((gain_stack, bias_stack), ("grp", "ctx", "wsh"))
    return (
        result,
        grad_input,
        summed_qkv,
        summed_out,
        summed_up,
        summed_down,
        gain_total,
        bias_total,
    )


def solution(mesh):
    return jax.shard_map(
        per_device,
        mesh=mesh,
        in_specs=(
            P("grp", "wsh", "ctx", None),
            P("wsh", None),
            P("wsh", None),
            P("wsh", None),
            P("wsh", None),
            P(),
            P(),
            P("grp", "wsh", "ctx", None),
            P("grp", "wsh", "ctx", None),
        ),
        out_specs=(
            P("grp", "wsh", "ctx", None),
            P("grp", "wsh", "ctx", None),
            P("wsh", None),
            P("wsh", None),
            P("wsh", None),
            P("wsh", None),
            P(),
            P(),
        ),
        check_vma=False,
    )
```

profile of v0, /device:TPU:0, one launch (start us, length us, event | category | flops | bytes accessed | tf_op | source)
XLA Modules:
  0.0 1249.4 jit_solution(280551970439620946)
XLA Ops:
  10.9 47.8 %all-gather.7.cloned.1.call-done = bf16[1024,3072]{1,0:T(8,128)(2,1)} async-done(((bf16[256,3072]{1,0:T(8,128)(2,1)}), bf16[1024,3072]{1,0:T(8,128)(2,1)}) %all-gather.7.cloned.1.call-update) | async-done | bytes 6291472 | tf_op jit(solution)/shard_map/all_gather | solution.py:155
  73.1 14.1 %all_gather.21 = s32[2048,2]{0,1:T(2,128)S(1)} all-gather(s32[512,2]{0,1:T(2,128)S(1)} %stack.6), channel_id=1, replica_groups=mesh['grp'=2,'ctx'=4,'wsh'=4] {'ctx'}, dimensions={0}, use_global_device_ids=true | all-gather | bytes 20480 | tf_op jit(solution)/shard_map/all_gather | solution.py:179
  92.5 57.1 %all-gather.9.cloned.1.call-done = bf16[2048,1024]{1,0:T(8,128)(2,1)} async-done(((bf16[512,1024]{1,0:T(8,128)(2,1)}), bf16[2048,1024]{1,0:T(8,128)(2,1)}) %all-gather.9.cloned.1.call-update) | async-done | bytes 4194320 | tf_op jit(solution)/shard_map/all_gather | solution.py:177
  169.2 10.0 copy.42
  179.2 52.0 %all-gather.11.cloned.1.call-done = bf16[2048,1024]{1,0:T(8,128)(2,1)} async-done(((bf16[512,1024]{1,0:T(8,128)(2,1)}), bf16[2048,1024]{1,0:T(8,128)(2,1)}) %all-gather.11.cloned.1.call-update) | async-done | bytes 4194320 | tf_op jit(solution)/shard_map/all_gather | solution.py:178
  231.1 11.7 reshape.274
  242.9 9.8 copy.44
  252.7 19.8 %while.59 = (s32[]{:T(128)}, f32[16,512]{1,0:T(8,128)S(1)}, f32[16,512]{1,0:T(8,128)S(1)}, s32[4,512,2]{1,2,0:T(2,128)S(1)}, s32[]{:T(128)}, /*index=5*/bf16[4,5...) while((s32[]{:T(128)}, f32[16,512]{1,0:T(8,128)S(1)}, ...), condition=%wide.region_8.9_spmd.clone, body=%wide.region_2.8_spmd.clone.sunk | while | flops 571230208 | bytes 36886224 | solution.py:76
  274.1 24.3 %while.60 = (s32[]{:T(128)}, f32[512,16,64]{0,2,1:T(8,128)}, s32[4,512,2]{1,2,0:T(2,128)S(1)}, s32[]{:T(128)}, bf16[4,512,16,64]{3,2,1,0:T(8,128)(2,1)}, /*index...) while((s32[]{:T(128)}, f32[512,16,64]{0,2,1:T(8,128)}, ...), condition=%wide.region_13.14_spmd.clone, body=%wide.region_9.13_spmd.clone.sunk | while | flops 1096026112 | bytes 11065027 | solution.py:76
  277.2 12.3 conditional.13
  279.2 10.3 bitcast_add_fusion
  313.4 13.1 %fusion.115 = f32[512,4096]{1,0:T(8,128)} fusion(bf16[1024,4096]{1,0:T(8,128)(2,1)} %all-gather.15.cloned.1.call-done, f32[512,1024]{1,0:T(8,128)} %copy-done.1, f32[1024]{0:T(1024)S(1)} %bitcast.299, f32[1024]{0:T(1024)S(1)} %bitcast.289, f32[512]{0:T(512)S(1)} %fusion.106, f32[512]{0:T(512)S(1)} %broadcast_multiply_fusion.1), kind=kOutput, calls=%fused_computation.179 | convolution fusion | flops 4297588736 | bytes 18886656 | tf_op jit(solution)/shard_map/dot_general | solution.py:200
  326.5 46.6 %all-gather.17.cloned.1.call-done = bf16[4096,1024]{1,0:T(8,128)(2,1)} async-done(((bf16[1024,1024]{1,0:T(8,128)(2,1)}), bf16[4096,1024]{1,0:T(8,128)(2,1)}) %all-gather.17.cloned.1.call-update) | async-done | bytes 8388624 | tf_op jit(solution)/shard_map/all_gather | solution.py:158
  373.2 10.5 fusion.130
  388.3 15.7 %fusion.80 = bf16[512,4096]{1,0:T(8,128)(2,1)} fusion(f32[512,4096]{1,0:T(8,128)} %fusion.115, bf16[4096,1024]{1,0:T(8,128)(2,1)} %all-gather.17.cloned.1.call-done, f32[512,1024]{1,0:T(8,128)S(1)} %get-tuple-element.761, f32[512]{0:T(512)S(1)} %negate_multiply_fusion.3), kind=kOutput, calls=%fused_computation.97 | convolution fusion | flops 4337958912 | bytes 23070720 | tf_op jit(solution)/shard_map/dot_general | solution.py:27
  419.4 22.5 %while.61 = (s32[]{:T(128)}, f32[16,512]{1,0:T(8,128)S(1)}, s32[4,512,2]{1,2,0:T(2,128)S(1)}, s32[]{:T(128)}, bf16[4,512,16,64]{1,3,2,0:T(8,128)(2,1)}, /*index=...) while((s32[]{:T(128)}, f32[16,512]{1,0:T(8,128)S(1)}, ...), condition=%wide.region_31.32_spmd.clone, body=%wide.region_26.31_spmd.clone.sunk | while | flops 1099696128 | bytes 38459600 | solution.py:76
  422.4 10.7 conditional.14
  443.2 68.5 %while.62 = (s32[]{:T(128)}, f32[512,16,64]{0,2,1:T(8,128)S(1)}, bf16[4,512,16,64]{1,3,2,0:T(8,128)(2,1)}, bf16[4,512,16,64]{1,3,2,0:T(8,128)(2,1)}, s32[4,512,2...) while((s32[]{:T(128)}, f32[512,16,64]{0,2,1:T(8,128)S(1)}, ...), condition=%wide.region_36.37_spmd.clone, body=%wide.region_32.0_spmd.clone.sunk | while | flops 2740193280 | bytes 94231808 | solution.py:76
  446.3 37.5 %conditional.15 = (f32[512,16,64]{0,2,1:T(8,128)S(1)}, bf16[1,512,16,64]{1,3,2,0:T(8,128)(2,1)}, bf16[1,512,16,64]{1,3,2,0:T(8,128)(2,1)}) conditional(s32[]{:T(128)} %convert_element_type.266, f32[512,16,64]{0,2,1:T(8,128)S(1)} %get-tuple-element.1188, (pred[512,512]{0,1:T(8,128)(4,1)S(1)}, bf16[4,512,16,64]{1,3,2,0:T(8,128)(2,1)}, s32[]{:T(128)}, ...), branch_computations={%region_34.34_spmd, %region_35.35_spmd} | conditional | flops 2739404800 | bytes 89753112 | solution.py:74
  446.3 9.3 fusion.59
  455.7 11.3 fusion.54
  467.0 10.5 fusion.46
  536.1 11.3 convolution_convert_fusion
  548.1 10.8 convolution_convert_fusion.1
  560.1 128.8 %reduce-scatter.9.cloned.1.call-done = bf16[512,1024]{0,1:T(8,128)(2,1)} async-done(((bf16[2048,1024]{0,1:T(8,128)(2,1)}), bf16[512,1024]{0,1:T(8,128)(2,1)}) %reduce-scatter.9.cloned.1.call-update) | async-done | bytes 1048592 | tf_op jit(solution)/shard_map/reduce_scatter | solution.py:237
  688.9 80.3 %reduce-scatter.7.cloned.1.call-done = bf16[512,1024]{0,1:T(8,128)(2,1)} async-done(((bf16[2048,1024]{0,1:T(8,128)(2,1)}), bf16[512,1024]{0,1:T(8,128)(2,1)}) %reduce-scatter.7.cloned.1.call-update) | async-done | bytes 1048592 | tf_op jit(solution)/shard_map/reduce_scatter | solution.py:234
  777.8 25.9 %reduce-scatter.13.cloned.1.call-done = bf16[256,1024]{1,0:T(8,128)(2,1)} async-done(((bf16[1024,1024]{1,0:T(8,128)(2,1)}), bf16[256,1024]{1,0:T(8,128)(2,1)}) %reduce-scatter.13.cloned.1.call-update) | async-done | bytes 524304 | tf_op jit(solution)/shard_map/reduce_scatter | solution.py:259
  803.7 74.4 %reduce-scatter.17.cloned.1.call-done = bf16[1024,1024]{1,0:T(8,128)(2,1)} async-done(((bf16[4096,1024]{1,0:T(8,128)(2,1)}), bf16[1024,1024]{1,0:T(8,128)(2,1)}) %reduce-scatter.17.cloned.1.call-update) | async-done | bytes 2097168 | tf_op jit(solution)/shard_map/reduce_scatter | solution.py:265
  878.1 74.4 %reduce-scatter.15.cloned.1.call-done = bf16[256,4096]{1,0:T(8,128)(2,1)} async-done(((bf16[1024,4096]{1,0:T(8,128)(2,1)}), bf16[256,4096]{1,0:T(8,128)(2,1)}) %reduce-scatter.15.cloned.1.call-update) | async-done | bytes 2097168 | tf_op jit(solution)/shard_map/reduce_scatter | solution.py:262
  952.4 60.9 %reduce-scatter.11.cloned.1.call-done = bf16[256,3072]{1,0:T(8,128)(2,1)} async-done(((bf16[1024,3072]{1,0:T(8,128)(2,1)}), bf16[256,3072]{1,0:T(8,128)(2,1)}) %reduce-scatter.11.cloned.1.call-update) | async-done | bytes 1572880 | tf_op jit(solution)/shard_map/reduce_scatter | solution.py:256
  1024.6 43.2 %all-reduce.1 = (f32[4,1024]{1,0:T(4,128)}, f32[4,1024]{1,0:T(4,128)}) all-reduce(f32[4,1024]{1,0:T(4,128)S(1)} %get-tuple-element.797, f32[4,1024]{1,0:T(4,128)S(1)} %get-tuple-element.798), channel_id=1, replica_groups=mesh['grp'=2,'ctx'=4,'wsh'=4] {'grp','ctx','wsh'}, use_global_device_ids=true, to_apply=%region_53.54 | all-reduce | flops 8192 | bytes 65536 | tf_op jit(solution)/shard_map/psum | solution.py:277
  1071.4 161.8 %all-reduce.5.cloned.1.call-done = (bf16[256,3072]{1,0:T(8,128)(2,1)}, bf16[256,1024]{1,0:T(8,128)(2,1)}, bf16[256,4096]{1,0:T(8,128)(2,1)}, bf16[1024,1024]{1,0:T(8,128)(2,1)}) async-done(((bf16[256,3072]{1,0:T(8,128)(2,1)}, bf16[256,1024]{1,0:T(8,128)(2,1)}, bf16[256,4096]{1,0:T(8,128)(2,1)}, bf16[1024,1024]{1,0:T(8,128)(2,1)}), (bf16[256,3072]{1,0:T(8,128)(2,1)}, bf16[256,1024]{1,0:T(8,128)(2,1)}, ...) | async-done | bytes 6291472 | tf_op jit(solution)/shard_map/psum | solution.py:270
  (318 shorter events, 236.0 us)
Async XLA Ops:
  7.2 51.5 %all-gather.7.cloned.1.call-start = ((), (), s32[]{:S(2)}) async-start(), calls=%async_computation.6 | async-start | bytes 7864320 | tf_op jit(solution)/shard_map/all_gather | solution.py:155
  7.9 141.7 %all-gather.9.cloned.1.call-start = ((), (), s32[]{:S(2)}) async-start(), calls=%async_computation.7 | async-start | bytes 5242880 | tf_op jit(solution)/shard_map/all_gather | solution.py:177
  8.6 58.4 %copy-start.22 = (f32[512]{0:T(512)}, f32[512]{0:T(512)S(1)}, u32[]{:S(2)}) copy-start(f32[512]{0:T(512)S(1)} %broadcast_multiply_fusion.3) | copy-start | bytes 6148
  9.6 57.4 %copy-start.28 = (f32[512]{0:T(512)}, f32[512]{0:T(512)S(1)}, u32[]{:S(2)}) copy-start(f32[512]{0:T(512)S(1)} %fusion.104) | copy-start | bytes 6148
  10.3 56.8 %copy-start.19 = (f32[1,1024]{1,0:T(1,128)}, f32[1,1024]{1,0:T(1,128)S(1)}, u32[]{:S(2)}) copy-start(f32[1,1024]{1,0:T(1,128)S(1)} %get-tuple-element.781) | copy-start | bytes 12292
  10.9 56.2 %copy-start.42 = (f32[1,1024]{1,0:T(1,128)}, f32[1,1024]{1,0:T(1,128)S(1)}, u32[]{:S(2)}) copy-start(f32[1,1024]{1,0:T(1,128)S(1)} %get-tuple-element.785) | copy-start | bytes 12292
  68.6 162.6 %all-gather.11.cloned.1.call-start = ((), (), s32[]{:S(2)}) async-start(), calls=%async_computation.8 | async-start | bytes 5242880 | tf_op jit(solution)/shard_map/all_gather | solution.py:178
  69.3 231.8 %all-gather.13.cloned.1.call-start = ((), (), s32[]{:S(2)}) async-start(), calls=%async_computation.9 | async-start | bytes 2621440 | tf_op jit(solution)/shard_map/all_gather | solution.py:156
  69.9 243.5 %all-gather.15.cloned.1.call-start = ((), (), s32[]{:S(2)}) async-start(), calls=%async_computation.10 | async-start | bytes 10485760 | tf_op jit(solution)/shard_map/all_gather | solution.py:157
  70.5 302.7 %all-gather.17.cloned.1.call-start = ((), (), s32[]{:S(2)}) async-start(), calls=%async_computation.11 | async-start | bytes 10485760 | tf_op jit(solution)/shard_map/all_gather | solution.py:158
  71.1 617.8 %reduce-scatter.9.cloned.1.call-start = ((), (), s32[]{:S(2)}) async-start(), calls=%async_computation.13 | async-start | bytes 5242880 | tf_op jit(solution)/shard_map/reduce_scatter | solution.py:237
  306.4 7.1 copy-start.36
  306.4 7.1 copy-start.44
  306.4 106.1 %copy-start.26 = (f32[512]{0:T(512)}, f32[512]{0:T(512)S(1)}, u32[]{:S(2)}) copy-start(f32[512]{0:T(512)S(1)} %broadcast_multiply_fusion.1) | copy-start | bytes 6148
  308.0 104.5 %copy-start.38 = (f32[512]{0:T(512)}, f32[512]{0:T(512)S(1)}, u32[]{:S(2)}) copy-start(f32[512]{0:T(512)S(1)} %fusion.106) | copy-start | bytes 6148
  386.3 17.7 %slice-start = ((s8[8388608]{0:T(1024)(128)(4,1)}), s8[4194304]{0:T(1024)(128)(4,1)S(1)}, s32[]{:S(2)}) async-start(s8[8388608]{0:T(1024)(128)(4,1)} %bitcast.301), calls=%async_computation.19 | async-start | bytes 8388608
  388.3 15.7 %copy-start.16 = (f32[512,1024]{1,0:T(8,128)}, f32[512,1024]{1,0:T(8,128)S(1)}, u32[]{:S(2)}) copy-start(f32[512,1024]{1,0:T(8,128)S(1)} %get-tuple-element.761) | copy-start | bytes 6291460
  388.3 15.7 %copy-start.46 = (f32[512]{0:T(512)}, f32[512]{0:T(512)S(1)}, u32[]{:S(2)}) copy-start(f32[512]{0:T(512)S(1)} %negate_multiply_fusion.3) | copy-start | bytes 6148
  388.3 15.7 %slice-start.1 = ((s8[8388608]{0:T(1024)(128)(4,1)}), s8[4194304]{0:T(1024)(128)(4,1)S(1)}, s32[]{:S(2)}) async-start(s8[8388608]{0:T(1024)(128)(4,1)} %bitcast.301), calls=%async_computation.20 | async-start | bytes 8388608
  520.8 248.4 %reduce-scatter.7.cloned.1.call-start = ((), (), s32[]{:S(2)}) async-start(), calls=%async_computation.12 | async-start | bytes 5242880 | tf_op jit(solution)/shard_map/reduce_scatter | solution.py:234
  530.0 273.7 %reduce-scatter.13.cloned.1.call-start = ((), (), s32[]{:S(2)}) async-start(), calls=%async_computation.15 | async-start | bytes 2621440 | tf_op jit(solution)/shard_map/reduce_scatter | solution.py:259
  535.5 342.6 %reduce-scatter.17.cloned.1.call-start = ((), (), s32[]{:S(2)}) async-start(), calls=%async_computation.17 | async-start | bytes 10485760 | tf_op jit(solution)/shard_map/reduce_scatter | solution.py:265
  547.5 405.0 %reduce-scatter.15.cloned.1.call-start = ((), (), s32[]{:S(2)}) async-start(), calls=%async_computation.16 | async-start | bytes 10485760 | tf_op jit(solution)/shard_map/reduce_scatter | solution.py:262
  558.9 210.3 %copy-start.5 = (bf16[1,1,512,1024]{3,2,1,0:T(8,128)(2,1)S(1)}, bf16[1,1,512,1024]{3,2,1,0:T(8,128)(2,1)}, u32[]{:S(2)}) copy-start(bf16[1,1,512,1024]{3,2,1,0:T(8,128)(2,1)} %param.25) | copy-start | bytes 3145732
  559.0 210.3 %copy-start.20 = (f32[1,1024]{1,0:T(1,128)S(1)}, f32[1,1024]{1,0:T(1,128)}, u32[]{:S(2)}) copy-start(f32[1,1024]{1,0:T(1,128)} %copy-done.19) | copy-start | bytes 12292
  559.0 210.2 %copy-start.23 = (f32[512]{0:T(512)S(1)}, f32[512]{0:T(512)}, u32[]{:S(2)}) copy-start(f32[512]{0:T(512)} %copy-done.22) | copy-start | bytes 6148
  559.0 210.2 %copy-start.29 = (f32[512]{0:T(512)S(1)}, f32[512]{0:T(512)}, u32[]{:S(2)}) copy-start(f32[512]{0:T(512)} %copy-done.28) | copy-start | bytes 6148
  559.0 210.2 %copy-start.43 = (f32[1,1024]{1,0:T(1,128)S(1)}, f32[1,1024]{1,0:T(1,128)}, u32[]{:S(2)}) copy-start(f32[1,1024]{1,0:T(1,128)} %copy-done.42) | copy-start | bytes 12292
  559.0 454.4 %reduce-scatter.11.cloned.1.call-start = ((), (), s32[]{:S(2)}) async-start(), calls=%async_computation.14 | async-start | bytes 7864320 | tf_op jit(solution)/shard_map/reduce_scatter | solution.py:256
  777.6 455.6 %all-reduce.5.cloned.1.call-start = ((), (), s32[]{:S(2)}) async-start(), calls=%async_computation.18 | async-start | bytes 12582912 | tf_op jit(solution)/shard_map/psum | solution.py:270
  1014.9 7.3 copy-start.25
  1022.2 45.6 %copy-start.7 = (f32[512,1024]{1,0:T(8,128)S(1)}, f32[512,1024]{1,0:T(8,128)}, u32[]{:S(2)}) copy-start(f32[512,1024]{1,0:T(8,128)} %copy-done.6) | copy-start | bytes 6291460
  (34 other events, 55.5 us)
Sparse Core Ops, SparseCore 0:
  9.6 49.0 all-gather.6
  68.7 80.8 all-gather.8
  151.8 79.3 all-gather.10
  232.5 21.1 all-gather.12
  255.1 58.2 all-gather.14
  314.8 58.2 all-gather.16
  520.9 167.9 reduce-scatter.8
  691.9 77.2 reduce-scatter.6
  771.7 31.9 reduce-scatter.12
  806.3 71.7 reduce-scatter.16
  880.7 71.7 reduce-scatter.14
  955.0 58.3 reduce-scatter.10
  1017.8 215.3 all-reduce.4
where the time goes:
time: 1250 us
  waiting for transfers between devices  818 us (65%)
  matrix products  165 us (13%)
  local copies, waits for them, and re-layouts  112 us (9%)
  other arithmetic  69.5 us (6%)
  blocking collectives  57.3 us (5%)
  between operations  14.7 us (1%)
    psum x1, waiting for transfers between devices, per_device(): lax.psum(shard_qkv.astype(jnp.bfloat16), ('grp', 'ctx')).astype(jnp.float32)  162 us
    reduce_scatter x1, waiting for transfers between devices, per_device(): lax.psum_scatter(value_terms.astype(jnp.bfloat16), 'ctx', scatter_dimensi...  129 us
    reduce_scatter x1, waiting for transfers between devices, per_device(): lax.psum_scatter(key_terms.astype(jnp.bfloat16), 'ctx', scatter_dimension...  80.3 us
    reduce_scatter x1, waiting for transfers between devices, per_device(): lax.psum_scatter(term_down.astype(jnp.bfloat16), 'wsh', scatter_dimension...  74.4 us
    reduce_scatter x1, waiting for transfers between devices, per_device(): lax.psum_scatter(term_up.astype(jnp.bfloat16), 'wsh', scatter_dimension=0...  74.4 us
    reduce_scatter x1, waiting for transfers between devices, per_device(): lax.psum_scatter(term_qkv.astype(jnp.bfloat16), 'wsh', scatter_dimension=...  60.9 us
    all_gather x1, waiting for transfers between devices, per_device(): lax.all_gather(key_local, 'ctx', axis=0, tiled=True)  57.1 us
    all_gather x1, waiting for transfers between devices, per_device(): lax.all_gather(value_local, 'ctx', axis=0, tiled=True)  52 us
  transfers between devices with their start and end apart: 13, of which 12 were waited for; matrix products, arithmetic and copies ran while one was open for 14% of the time, Pallas kernels for 0%

commit v1 on v0

--- a/solution.py
+++ b/solution.py
@@ -267,7 +267,9 @@
         ).astype(jnp.float32),
     )
     summed_qkv, summed_out, summed_up, summed_down = (
-        lax.psum(shard_qkv.astype(jnp.bfloat16), ("grp", "ctx")).astype(jnp.float32),
+        jnp.sum(lax.all_gather(shard_qkv.astype(jnp.bfloat16), ("grp", "ctx")), axis=0).astype(
+            jnp.float32
+        ),
         lax.psum(shard_out.astype(jnp.bfloat16), ("grp", "ctx")).astype(jnp.float32),
         lax.psum(shard_up.astype(jnp.bfloat16), ("grp", "ctx")).astype(jnp.float32),
         lax.psum(shard_down.astype(jnp.bfloat16), ("grp", "ctx")).astype(jnp.float32),

time: 1250 us -> 1390 us (1.11)
  waiting for transfers between devices: 818 us -> 942 us
    all_gather x0 -> x1, waiting for transfers between devices: none -> 168 us  [per_device(): lax.all_gather(shard_qkv.astype(jnp.bfloat16), ('grp', 'ctx'))]
    psum x1, waiting for transfers between devices: 162 us -> 117 us  [per_device(): lax.psum(shard_out.astype(jnp.bfloat16), ('grp', 'ctx')).astype(jnp.float32)]
    unnamed x112 -> x108, local copies, waits for them, and re-layouts: 46.7 us -> 45.2 us
  transfers between devices with their start and end apart: 13 -> 14, of which waited for: 12 -> 13; matrix products, arithmetic and copies ran while one was open for 14% -> 13% of each run, Pallas kernels for 0% -> 0%
where the time goes in v1:
time: 1390 us; the launch traced here: 1380 us
  waiting for transfers between devices  942 us (68%)
  matrix products  165 us (12%)
  local copies, waits for them, and re-layouts  111 us (8%)
  other arithmetic  77.9 us (6%)
  blocking collectives  59.4 us (4%)
  between operations  14.8 us (1%)
    all_gather x1, waiting for transfers between devices, per_device(): lax.all_gather(shard_qkv.astype(jnp.bfloat16), ('grp', 'ctx'))  168 us
    reduce_scatter x1, waiting for transfers between devices, per_device(): lax.psum_scatter(value_terms.astype(jnp.bfloat16), 'ctx', scatter_dimensi...  129 us
    psum x1, waiting for transfers between devices, per_device(): lax.psum(shard_out.astype(jnp.bfloat16), ('grp', 'ctx')).astype(jnp.float32)  117 us
    reduce_scatter x1, waiting for transfers between devices, per_device(): lax.psum_scatter(key_terms.astype(jnp.bfloat16), 'ctx', scatter_dimension...  80.3 us
    reduce_scatter x1, waiting for transfers between devices, per_device(): lax.psum_scatter(term_up.astype(jnp.bfloat16), 'wsh', scatter_dimension=0...  74.4 us
    reduce_scatter x1, waiting for transfers between devices, per_device(): lax.psum_scatter(term_down.astype(jnp.bfloat16), 'wsh', scatter_dimension...  74.3 us
    reduce_scatter x1, waiting for transfers between devices, per_device(): lax.psum_scatter(term_qkv.astype(jnp.bfloat16), 'wsh', scatter_dimension=...  60.7 us
    all_gather x1, waiting for transfers between devices, per_device(): lax.all_gather(key_local, 'ctx', axis=0, tiled=True)  57.1 us
  transfers between devices with their start and end apart: 14, of which 13 were waited for; matrix products, arithmetic and copies ran while one was open for 13% of the time, Pallas kernels for 0%

profile of v1, /device:TPU:0, one launch (start us, length us, event | category | flops | bytes accessed | tf_op | source)
XLA Modules:
  0.0 1381.4 jit_solution(14990254059145719077)
XLA Ops:
  10.9 47.8 %all-gather.9.cloned.1.call-done = bf16[1024,3072]{1,0:T(8,128)(2,1)} async-done(((bf16[256,3072]{1,0:T(8,128)(2,1)}), bf16[1024,3072]{1,0:T(8,128)(2,1)}) %all-gather.9.cloned.1.call-update) | async-done | bytes 6291472 | tf_op jit(solution)/shard_map/all_gather | solution.py:155
  73.1 14.2 %all_gather.27 = s32[2048,2]{0,1:T(2,128)S(1)} all-gather(s32[512,2]{0,1:T(2,128)S(1)} %stack.6), channel_id=1, replica_groups=mesh['grp'=2,'ctx'=4,'wsh'=4] {'ctx'}, dimensions={0}, use_global_device_ids=true | all-gather | bytes 20480 | tf_op jit(solution)/shard_map/all_gather | solution.py:179
  92.5 57.1 %all-gather.11.cloned.1.call-done = bf16[2048,1024]{1,0:T(8,128)(2,1)} async-done(((bf16[512,1024]{1,0:T(8,128)(2,1)}), bf16[2048,1024]{1,0:T(8,128)(2,1)}) %all-gather.11.cloned.1.call-update) | async-done | bytes 4194320 | tf_op jit(solution)/shard_map/all_gather | solution.py:177
  169.2 10.0 copy.42
  179.2 52.0 %all-gather.13.cloned.1.call-done = bf16[2048,1024]{1,0:T(8,128)(2,1)} async-done(((bf16[512,1024]{1,0:T(8,128)(2,1)}), bf16[2048,1024]{1,0:T(8,128)(2,1)}) %all-gather.13.cloned.1.call-update) | async-done | bytes 4194320 | tf_op jit(solution)/shard_map/all_gather | solution.py:178
  231.1 11.7 reshape.275
  242.9 9.8 copy.44
  252.7 19.8 %while.59 = (s32[]{:T(128)}, f32[16,512]{1,0:T(8,128)S(1)}, f32[16,512]{1,0:T(8,128)S(1)}, s32[4,512,2]{1,2,0:T(2,128)S(1)}, s32[]{:T(128)}, /*index=5*/bf16[4,5...) while((s32[]{:T(128)}, f32[16,512]{1,0:T(8,128)S(1)}, ...), condition=%wide.region_8.9_spmd.clone, body=%wide.region_2.8_spmd.clone.sunk | while | flops 571230208 | bytes 36886224 | solution.py:76
  274.1 24.2 %while.60 = (s32[]{:T(128)}, f32[512,16,64]{0,2,1:T(8,128)}, s32[4,512,2]{1,2,0:T(2,128)S(1)}, s32[]{:T(128)}, bf16[4,512,16,64]{3,2,1,0:T(8,128)(2,1)}, /*index...) while((s32[]{:T(128)}, f32[512,16,64]{0,2,1:T(8,128)}, ...), condition=%wide.region_13.14_spmd.clone, body=%wide.region_9.13_spmd.clone.sunk | while | flops 1096026112 | bytes 11065027 | solution.py:76
  277.2 12.3 conditional.13
  279.1 10.3 bitcast_add_fusion
  313.4 13.1 fusion.115
  326.6 46.6 %all-gather.19.cloned.1.call-done = bf16[4096,1024]{1,0:T(8,128)(2,1)} async-done(((bf16[1024,1024]{1,0:T(8,128)(2,1)}), bf16[4096,1024]{1,0:T(8,128)(2,1)}) %all-gather.19.cloned.1.call-update) | async-done | bytes 8388624 | tf_op jit(solution)/shard_map/all_gather | solution.py:158
  373.2 10.5 fusion.130
  388.3 15.6 %fusion.80 = bf16[512,4096]{1,0:T(8,128)(2,1)} fusion(f32[512,4096]{1,0:T(8,128)} %fusion.115, bf16[4096,1024]{1,0:T(8,128)(2,1)} %all-gather.19.cloned.1.call-done, f32[512,1024]{1,0:T(8,128)S(1)} %get-tuple-element.760, f32[512]{0:T(512)S(1)} %negate_multiply_fusion.3), kind=kOutput, calls=%fused_computation.97 | convolution fusion | flops 4337958912 | bytes 23070720 | tf_op jit(solution)/shard_map/dot_general | solution.py:27
  419.4 22.1 %while.61 = (s32[]{:T(128)}, f32[16,512]{1,0:T(8,128)S(1)}, s32[4,512,2]{1,2,0:T(2,128)S(1)}, s32[]{:T(128)}, bf16[4,512,16,64]{1,3,2,0:T(8,128)(2,1)}, /*index=...) while((s32[]{:T(128)}, f32[16,512]{1,0:T(8,128)S(1)}, ...), condition=%wide.region_31.32_spmd.clone, body=%wide.region_26.31_spmd.clone.sunk | while | flops 1099696128 | bytes 38459600 | solution.py:76
  422.2 10.7 conditional.14
  442.7 68.3 %while.62 = (s32[]{:T(128)}, f32[512,16,64]{0,2,1:T(8,128)S(1)}, bf16[4,512,16,64]{1,3,2,0:T(8,128)(2,1)}, bf16[4,512,16,64]{1,3,2,0:T(8,128)(2,1)}, s32[4,512,2...) while((s32[]{:T(128)}, f32[512,16,64]{0,2,1:T(8,128)S(1)}, ...), condition=%wide.region_36.37_spmd.clone, body=%wide.region_32.0_spmd.clone.sunk | while | flops 2740193280 | bytes 94231808 | solution.py:76
  445.8 37.6 %conditional.15 = (f32[512,16,64]{0,2,1:T(8,128)S(1)}, bf16[1,512,16,64]{1,3,2,0:T(8,128)(2,1)}, bf16[1,512,16,64]{1,3,2,0:T(8,128)(2,1)}) conditional(s32[]{:T(128)} %convert_element_type.268, f32[512,16,64]{0,2,1:T(8,128)S(1)} %get-tuple-element.1187, (pred[512,512]{0,1:T(8,128)(4,1)S(1)}, bf16[4,512,16,64]{1,3,2,0:T(8,128)(2,1)}, s32[]{:T(128)}, ...), branch_computations={%region_34.34_spmd, %region_35.35_spmd} | conditional | flops 2739404800 | bytes 89753112 | solution.py:74
  455.1 11.3 fusion.54
  466.4 10.5 fusion.46
  535.5 11.3 convolution_convert_fusion
  547.5 10.8 convolution_convert_fusion.1
  559.5 128.8 %reduce-scatter.9.cloned.1.call-done = bf16[512,1024]{0,1:T(8,128)(2,1)} async-done(((bf16[2048,1024]{0,1:T(8,128)(2,1)}), bf16[512,1024]{0,1:T(8,128)(2,1)}) %reduce-scatter.9.cloned.1.call-update) | async-done | bytes 1048592 | tf_op jit(solution)/shard_map/reduce_scatter | solution.py:237
  688.3 80.3 %reduce-scatter.7.cloned.1.call-done = bf16[512,1024]{0,1:T(8,128)(2,1)} async-done(((bf16[2048,1024]{0,1:T(8,128)(2,1)}), bf16[512,1024]{0,1:T(8,128)(2,1)}) %reduce-scatter.7.cloned.1.call-update) | async-done | bytes 1048592 | tf_op jit(solution)/shard_map/reduce_scatter | solution.py:234
  777.0 26.1 %reduce-scatter.13.cloned.1.call-done = bf16[256,1024]{1,0:T(8,128)(2,1)} async-done(((bf16[1024,1024]{1,0:T(8,128)(2,1)}), bf16[256,1024]{1,0:T(8,128)(2,1)}) %reduce-scatter.13.cloned.1.call-update) | async-done | bytes 524304 | tf_op jit(solution)/shard_map/reduce_scatter | solution.py:259
  803.1 74.3 %reduce-scatter.17.cloned.1.call-done = bf16[1024,1024]{1,0:T(8,128)(2,1)} async-done(((bf16[4096,1024]{1,0:T(8,128)(2,1)}), bf16[1024,1024]{1,0:T(8,128)(2,1)}) %reduce-scatter.17.cloned.1.call-update) | async-done | bytes 2097168 | tf_op jit(solution)/shard_map/reduce_scatter | solution.py:265
  877.4 74.4 %reduce-scatter.15.cloned.1.call-done = bf16[256,4096]{1,0:T(8,128)(2,1)} async-done(((bf16[1024,4096]{1,0:T(8,128)(2,1)}), bf16[256,4096]{1,0:T(8,128)(2,1)}) %reduce-scatter.15.cloned.1.call-update) | async-done | bytes 2097168 | tf_op jit(solution)/shard_map/reduce_scatter | solution.py:262
  952.1 60.7 %reduce-scatter.11.cloned.1.call-done = bf16[256,3072]{1,0:T(8,128)(2,1)} async-done(((bf16[1024,3072]{1,0:T(8,128)(2,1)}), bf16[256,3072]{1,0:T(8,128)(2,1)}) %reduce-scatter.11.cloned.1.call-update) | async-done | bytes 1572880 | tf_op jit(solution)/shard_map/reduce_scatter | solution.py:256
  1022.7 45.2 %all-reduce.1 = (f32[4,1024]{1,0:T(4,128)}, f32[4,1024]{1,0:T(4,128)}) all-reduce(f32[4,1024]{1,0:T(4,128)S(1)} %get-tuple-element.796, f32[4,1024]{1,0:T(4,128)S(1)} %get-tuple-element.797), channel_id=1, replica_groups=mesh['grp'=2,'ctx'=4,'wsh'=4] {'grp','ctx','wsh'}, use_global_device_ids=true, to_apply=%region_53.54 | all-reduce | flops 8192 | bytes 65536 | tf_op jit(solution)/shard_map/psum | solution.py:279
  1071.5 116.6 %all-reduce.5.cloned.1.call-done = (bf16[256,1024]{1,0:T(8,128)(2,1)}, bf16[256,4096]{1,0:T(8,128)(2,1)}, bf16[1024,1024]{1,0:T(8,128)(2,1)}) async-done(((bf16[256,1024]{1,0:T(8,128)(2,1)}, bf16[256,4096]{1,0:T(8,128)(2,1)}, bf16[1024,1024]{1,0:T(8,128)(2,1)}), (bf16[256,1024]{1,0:T(8,128)(2,1)}, bf16[256,4096]{1,0:T(8,128)(2,1)}, bf16[1024,1024]{1,0:T(8,128)(2,1)})) %all-reduce.5.cloned.1.call-update) | async-done | bytes 4718608 | tf_op jit(solution)/shard_map/psum | solution.py:273
  1197.0 168.4 %all-gather.21.cloned.1.call-done = bf16[2048,3072]{1,0:T(8,128)(2,1)} async-done(((bf16[256,3072]{1,0:T(8,128)(2,1)}), bf16[2048,3072]{1,0:T(8,128)(2,1)}) %all-gather.21.cloned.1.call-update) | async-done | bytes 12582928 | tf_op jit(solution)/shard_map/all_gather | solution.py:270
  (318 shorter events, 252.6 us)
Async XLA Ops:
  7.2 51.5 %all-gather.9.cloned.1.call-start = ((), (), s32[]{:S(2)}) async-start(), calls=%async_computation.6 | async-start | bytes 7864320 | tf_op jit(solution)/shard_map/all_gather | solution.py:155
  7.9 141.7 %all-gather.11.cloned.1.call-start = ((), (), s32[]{:S(2)}) async-start(), calls=%async_computation.7 | async-start | bytes 5242880 | tf_op jit(solution)/shard_map/all_gather | solution.py:177
  8.6 58.4 %copy-start.20 = (f32[512]{0:T(512)}, f32[512]{0:T(512)S(1)}, u32[]{:S(2)}) copy-start(f32[512]{0:T(512)S(1)} %broadcast_multiply_fusion.3) | copy-start | bytes 6148
  9.6 57.4 %copy-start.26 = (f32[512]{0:T(512)}, f32[512]{0:T(512)S(1)}, u32[]{:S(2)}) copy-start(f32[512]{0:T(512)S(1)} %fusion.104) | copy-start | bytes 6148
  10.3 56.8 %copy-start.17 = (f32[1,1024]{1,0:T(1,128)}, f32[1,1024]{1,0:T(1,128)S(1)}, u32[]{:S(2)}) copy-start(f32[1,1024]{1,0:T(1,128)S(1)} %get-tuple-element.780) | copy-start | bytes 12292
  10.9 56.2 %copy-start.40 = (f32[1,1024]{1,0:T(1,128)}, f32[1,1024]{1,0:T(1,128)S(1)}, u32[]{:S(2)}) copy-start(f32[1,1024]{1,0:T(1,128)S(1)} %get-tuple-element.784) | copy-start | bytes 12292
  68.6 162.5 %all-gather.13.cloned.1.call-start = ((), (), s32[]{:S(2)}) async-start(), calls=%async_computation.8 | async-start | bytes 5242880 | tf_op jit(solution)/shard_map/all_gather | solution.py:178
  69.3 231.7 %all-gather.15.cloned.1.call-start = ((), (), s32[]{:S(2)}) async-start(), calls=%async_computation.9 | async-start | bytes 2621440 | tf_op jit(solution)/shard_map/all_gather | solution.py:156
  69.9 243.5 %all-gather.17.cloned.1.call-start = ((), (), s32[]{:S(2)}) async-start(), calls=%async_computation.10 | async-start | bytes 10485760 | tf_op jit(solution)/shard_map/all_gather | solution.py:157
  70.5 302.7 %all-gather.19.cloned.1.call-start = ((), (), s32[]{:S(2)}) async-start(), calls=%async_computation.11 | async-start | bytes 10485760 | tf_op jit(solution)/shard_map/all_gather | solution.py:158
  71.1 617.2 %reduce-scatter.9.cloned.1.call-start = ((), (), s32[]{:S(2)}) async-start(), calls=%async_computation.13 | async-start | bytes 5242880 | tf_op jit(solution)/shard_map/reduce_scatter | solution.py:237
  306.3 106.1 %copy-start.24 = (f32[512]{0:T(512)}, f32[512]{0:T(512)S(1)}, u32[]{:S(2)}) copy-start(f32[512]{0:T(512)S(1)} %broadcast_multiply_fusion.1) | copy-start | bytes 6148
  307.9 104.5 %copy-start.36 = (f32[512]{0:T(512)}, f32[512]{0:T(512)S(1)}, u32[]{:S(2)}) copy-start(f32[512]{0:T(512)S(1)} %fusion.106) | copy-start | bytes 6148
  386.4 17.6 %slice-start = ((s8[8388608]{0:T(1024)(128)(4,1)}), s8[4194304]{0:T(1024)(128)(4,1)S(1)}, s32[]{:S(2)}) async-start(s8[8388608]{0:T(1024)(128)(4,1)} %bitcast.303), calls=%async_computation.20 | async-start | bytes 8388608
  388.3 15.6 %copy-start.15 = (f32[512,1024]{1,0:T(8,128)}, f32[512,1024]{1,0:T(8,128)S(1)}, u32[]{:S(2)}) copy-start(f32[512,1024]{1,0:T(8,128)S(1)} %get-tuple-element.760) | copy-start | bytes 6291460
  388.3 15.6 %copy-start.44 = (f32[512]{0:T(512)}, f32[512]{0:T(512)S(1)}, u32[]{:S(2)}) copy-start(f32[512]{0:T(512)S(1)} %negate_multiply_fusion.3) | copy-start | bytes 6148
  388.3 15.6 %slice-start.1 = ((s8[8388608]{0:T(1024)(128)(4,1)}), s8[4194304]{0:T(1024)(128)(4,1)S(1)}, s32[]{:S(2)}) async-start(s8[8388608]{0:T(1024)(128)(4,1)} %bitcast.303), calls=%async_computation.21 | async-start | bytes 8388608
  520.2 248.4 %reduce-scatter.7.cloned.1.call-start = ((), (), s32[]{:S(2)}) async-start(), calls=%async_computation.12 | async-start | bytes 5242880 | tf_op jit(solution)/shard_map/reduce_scatter | solution.py:234
  529.4 273.7 %reduce-scatter.13.cloned.1.call-start = ((), (), s32[]{:S(2)}) async-start(), calls=%async_computation.15 | async-start | bytes 2621440 | tf_op jit(solution)/shard_map/reduce_scatter | solution.py:259
  534.8 342.6 %reduce-scatter.17.cloned.1.call-start = ((), (), s32[]{:S(2)}) async-start(), calls=%async_computation.17 | async-start | bytes 10485760 | tf_op jit(solution)/shard_map/reduce_scatter | solution.py:265
  546.9 404.9 %reduce-scatter.15.cloned.1.call-start = ((), (), s32[]{:S(2)}) async-start(), calls=%async_computation.16 | async-start | bytes 10485760 | tf_op jit(solution)/shard_map/reduce_scatter | solution.py:262
  558.3 210.2 %copy-start.5 = (bf16[1,1,512,1024]{3,2,1,0:T(8,128)(2,1)S(1)}, bf16[1,1,512,1024]{3,2,1,0:T(8,128)(2,1)}, u32[]{:S(2)}) copy-start(bf16[1,1,512,1024]{3,2,1,0:T(8,128)(2,1)} %param.25) | copy-start | bytes 3145732
  558.3 210.2 %copy-start.18 = (f32[1,1024]{1,0:T(1,128)S(1)}, f32[1,1024]{1,0:T(1,128)}, u32[]{:S(2)}) copy-start(f32[1,1024]{1,0:T(1,128)} %copy-done.17) | copy-start | bytes 12292
  558.4 210.2 %copy-start.21 = (f32[512]{0:T(512)S(1)}, f32[512]{0:T(512)}, u32[]{:S(2)}) copy-start(f32[512]{0:T(512)} %copy-done.20) | copy-start | bytes 6148
  558.4 210.2 %copy-start.27 = (f32[512]{0:T(512)S(1)}, f32[512]{0:T(512)}, u32[]{:S(2)}) copy-start(f32[512]{0:T(512)} %copy-done.26) | copy-start | bytes 6148
  558.4 210.2 %copy-start.41 = (f32[1,1024]{1,0:T(1,128)S(1)}, f32[1,1024]{1,0:T(1,128)}, u32[]{:S(2)}) copy-start(f32[1,1024]{1,0:T(1,128)} %copy-done.40) | copy-start | bytes 12292
  558.4 454.4 %reduce-scatter.11.cloned.1.call-start = ((), (), s32[]{:S(2)}) async-start(), calls=%async_computation.14 | async-start | bytes 7864320 | tf_op jit(solution)/shard_map/reduce_scatter | solution.py:256
  776.9 411.1 %all-reduce.5.cloned.1.call-start = ((), (), s32[]{:S(2)}) async-start(), calls=%async_computation.19 | async-start | bytes 9437184 | tf_op jit(solution)/shard_map/psum | solution.py:273
  951.8 61.0 %copy-start.9 = (bf16[1,1,512,1024]{3,2,1,0:T(8,128)(2,1)S(1)}, bf16[1,1,512,1024]{3,2,1,0:T(8,128)(2,1)}, u32[]{:S(2)}) copy-start(bf16[1,1,512,1024]{3,2,1,0:T(8,128)(2,1)} %param.33) | copy-start | bytes 3145732
  951.8 61.2 %copy-start.16 = (bf16[512,16,64]{0,2,1:T(8,128)(2,1)S(1)}, bf16[512,16,64]{0,2,1:T(8,128)(2,1)}, u32[]{:S(2)}) copy-start(bf16[512,16,64]{0,2,1:T(8,128)(2,1)} %convert_multiply_fusion) | copy-start | bytes 3145732
  951.8 413.6 %all-gather.21.cloned.1.call-start = ((), (), s32[]{:S(2)}) async-start(), calls=%async_computation.18 | async-start | bytes 14155776 | tf_op jit(solution)/shard_map/all_gather | solution.py:270
  1020.3 47.6 %copy-start.7 = (f32[512,1024]{1,0:T(8,128)S(1)}, f32[512,1024]{1,0:T(8,128)}, u32[]{:S(2)}) copy-start(f32[512,1024]{1,0:T(8,128)} %copy-done.6) | copy-start | bytes 6291460
  (33 other events, 71.8 us)
Sparse Core Ops, SparseCore 0:
  9.6 49.0 all-gather.8
  68.7 80.8 all-gather.10
  151.8 79.3 all-gather.12
  232.6 21.1 all-gather.14
  255.1 58.2 all-gather.16
  314.9 58.2 all-gather.18
  520.3 167.9 reduce-scatter.8
  691.3 77.2 reduce-scatter.6
  771.1 31.9 reduce-scatter.12
  805.7 71.6 reduce-scatter.16
  880.0 71.7 reduce-scatter.14
  954.3 58.3 reduce-scatter.10
  1016.7 171.2 all-reduce.4
  1190.0 175.3 all-gather.20
